TPU v7x, 256 devices: a whole 4x4x8 slice. The times are simulated.
256 devices in a mesh: row: 8 (over z), col: 16 (over x_hi, y, core), rep: 2 (over x_lo).
Axes of the slice: x: 4 (x_hi: 2, x_lo: 2; x = x_hi * 2 + x_lo), y: 4, z: 8, core: 2. Of those that a mesh axis runs over, the one named last changes fastest.
Arguments:
- descriptors: float32 [2048, 256], P('rep', 'col'), may hold values from -6 to 6
- landmarks: float32 [12288, 256], P('row', 'col'), may hold values from -6 to 6
- whitening: float32 [12288, 12288], P('row', 'col'), may hold values from -1 to 1
- assign: int32 [2048], replicated, may hold values from 0 to 4095
Outputs:
- cluster_sums: float32 [4096, 12288], P(('row', 'rep'), 'col')
All inputs are finite; a program needn't handle non-finite values.
Results may differ from a plain program's by a relative error of at most 0.00016.
Values sent between devices are 32-bit elements; how exact they have to be, the bound alone decides.
A program may use at most 64 MiB of HBM per device.

v0:
```python
import jax
import jax.numpy as jnp
from jax import lax
from jax.sharding import PartitionSpec as P

SPREAD = 51
CLUSTERS = 4096


highest = lax.Precision.HIGHEST


def kernel_tile(points, centres):
    row_square = jnp.sum(points * points, axis=1)
    centre_square = jnp.sum(centres * centres, axis=1)
    inner = jnp.dot(points, centres.T, precision=highest, preferred_element_type=jnp.float32)
    distance = row_square[:, None] + centre_square[None, :] - 2.0 * inner
    return jnp.exp(-distance / (2.0 * SPREAD))


def per_device(descriptors, landmarks, whitening, assign):
    part_rows = descriptors.shape[0]
    rep_position = lax.axis_index("rep")
    full_points, full_centres = (
        lax.all_gather(descriptors, "col", axis=1, tiled=True),
        lax.all_gather(landmarks, "col", axis=1, tiled=True),
    )
    kernel = kernel_tile(full_points, full_centres)
    whitened = jnp.dot(kernel, whitening, precision=highest, preferred_element_type=jnp.float32)
    owned_count = CLUSTERS // (lax.axis_size("row") * lax.axis_size("rep"))
    local_assign = lax.dynamic_slice_in_dim(assign, rep_position * part_rows, part_rows)
    labels = jnp.arange(owned_count * lax.axis_size(("row", "rep")), dtype=jnp.int32)
    onehot = (labels[:, None] == local_assign[None, :]).astype(jnp.float32)
    return lax.psum_scatter(
        jnp.dot(onehot, whitened, precision=highest, preferred_element_type=jnp.float32),
        ("row", "rep"),
        scatter_dimension=0,
        tiled=True,
    )


def solution(mesh):
    placed = (P("rep", "col"), P("row", "col"), P("row", "col"), P())
    return jax.shard_map(
        per_device, mesh=mesh, in_specs=placed, out_specs=P(("row", "rep"), "col"), check_vma=False
    )
```

profile of v0, /device:TPU:1, one launch (start us, length us, event | category | flops | bytes accessed | tf_op | source)
XLA Modules:
  0.0 440.5 jit_solution(17535972358049037863)
XLA Ops:
  6.5 0.0 all-gather.3.cloned.1.call-start
  6.5 0.7 all-gather.3.cloned.1.call-update
  7.3 0.0 all-gather.5.cloned.1.call-start
  7.3 0.7 all-gather.5.cloned.1.call-update
  8.0 0.0 reduce-scatter.2.cloned.1.call-start
  8.1 56.2 %all-gather.3.cloned.1.call-done = f32[1024,256]{0,1:T(8,128)} async-done(((f32[1024,16]{0,1:T(8,128)}), f32[1024,256]{0,1:T(8,128)}) %all-gather.3.cloned.1.call-update) | async-done | bytes 1048592 | tf_op jit(solution)/shard_map/all_gather | solution.py:25
  64.2 1.3 multiply_reduce_fusion.1
  65.6 51.5 %all-gather.5.cloned.1.call-done = f32[1536,256]{0,1:T(8,128)} async-done(((f32[1536,16]{0,1:T(8,128)}), f32[1536,256]{0,1:T(8,128)}) %all-gather.5.cloned.1.call-update) | async-done | bytes 1572880 | tf_op jit(solution)/shard_map/all_gather | solution.py:26
  117.1 0.0 slice-start
  117.1 1.7 multiply_reduce_fusion
  118.8 0.0 slice-start.1
  118.8 7.3 %fusion.15 = f32[1024,1536]{1,0:T(8,128)S(1)} fusion(f32[1024,256]{0,1:T(8,128)} %all-gather.3.cloned.1.call-done, f32[1536,256]{0,1:T(8,128)} %all-gather.5.cloned.1.call-done), kind=kOutput, calls=%fused_computation.18 | convolution fusion | flops 4831838208 | bytes 8912896 | tf_op jit(solution)/shard_map/dot_general | solution.py:16
  126.1 0.0 slice-done
  126.2 0.0 slice-done.1
  126.2 0.0 dynamic-slice-start
  126.2 16.3 %fusion.2 = f32[1024,768]{1,0:T(8,128)S(1)} fusion(f32[1536,768]{1,0:T(8,128)S(1)} %bitcast.5, f32[1024,1536]{1,0:T(8,128)S(1)} %fusion.15, f32[1536]{0:T(1024)S(1)} %multiply_reduce_fusion, f32[1024]{0:T(1024)S(1)} %multiply_reduce_fusion.1), kind=kOutput, calls=%fused_computation.3 | convolution fusion | flops 14503378944 | bytes 14166016 | tf_op jit(solution)/shard_map/dot_general | solution.py:29
  142.5 0.0 dynamic-slice-done
  142.5 25.8 %fusion = f32[4096,768]{1,0:T(8,128)} fusion(f32[1024,768]{1,0:T(8,128)S(1)} %fusion.2, s32[1024]{0:T(1024)S(1)} %dynamic-slice-done), kind=kOutput, calls=%fused_computation.1 | convolution fusion | flops 38658899968 | bytes 15732736 | tf_op jit(solution)/shard_map/dot_general | solution.py:35
  168.3 0.0 reduce-scatter.2.cloned.1.call-update
  168.3 265.7 %reduce-scatter.2.cloned.1.call-done = f32[256,768]{1,0:T(8,128)} async-done(((f32[4096,768]{1,0:T(8,128)}), f32[256,768]{1,0:T(8,128)}) %reduce-scatter.2.cloned.1.call-update) | async-done | bytes 786448 | tf_op jit(solution)/shard_map/reduce_scatter | solution.py:34
  (1 shorter events, 0.0 us)
Async XLA Ops:
  6.5 57.7 %all-gather.3.cloned.1.call-start = ((), (), s32[]{:S(2)}) async-start(), calls=%async_computation.1 | async-start | bytes 1114112 | tf_op jit(solution)/shard_map/all_gather | solution.py:25
  7.3 109.8 %all-gather.5.cloned.1.call-start = ((), (), s32[]{:S(2)}) async-start(), calls=%async_computation.2 | async-start | bytes 1671168 | tf_op jit(solution)/shard_map/all_gather | solution.py:26
  8.0 426.0 %reduce-scatter.2.cloned.1.call-start = ((), (), s32[]{:S(2)}) async-start(), calls=%async_computation.3 | async-start | bytes 13369344 | tf_op jit(solution)/shard_map/reduce_scatter | solution.py:34
  117.1 9.0 %slice-start = ((s8[4718592]{0:T(1024)(128)(4,1)}), s8[4194304]{0:T(1024)(128)(4,1)S(1)}, s32[]{:S(2)}) async-start(s8[4718592]{0:T(1024)(128)(4,1)} %bitcast.4), calls=%async_computation.5 | async-start | bytes 8388608
  118.8 7.4 %slice-start.1 = ((s8[4718592]{0:T(1024)(128)(4,1)}), s8[524288]{0:T(1024)(128)(4,1)S(1)}, s32[]{:S(2)}) async-start(s8[4718592]{0:T(1024)(128)(4,1)} %bitcast.4), calls=%async_computation.6 | async-start | bytes 1048576
  126.2 16.3 %dynamic-slice-start = ((s32[2048]{0:T(1024)}, s32[]{:T(128)}), s32[1024]{0:T(1024)S(1)}, s32[]{:S(2)}) async-start(s32[2048]{0:T(1024)} %param.7, s32[]{:T(128)} %select_n.3), calls=%async_computation.4 | async-start | bytes 8704 | tf_op jit(solution)/shard_map/dynamic_slice | solution.py:31
Sparse Core Ops, SparseCore 0:
  10.1 54.0 all-gather.2
  67.0 50.0 all-gather.4
  168.4 265.5 reduce-scatter.1
where the time goes:
time: 441 us
  waiting for transfers between devices  375 us (85%)
  matrix products  49.4 us (11%)
  between operations  13.2 us (3%)
    reduce_scatter x1, waiting for transfers between devices, per_device(): lax.psum_scatter(jnp.dot(onehot, whitened, precision=highest, preferred_e...  266 us
    all_gather x1, waiting for transfers between devices, per_device(): lax.all_gather(descriptors, 'col', axis=1, tiled=True)  56.2 us
    all_gather x1, waiting for transfers between devices, per_device(): lax.all_gather(landmarks, 'col', axis=1, tiled=True)  51.5 us
    dot_general x1, matrix products, per_device(): jnp.dot(onehot, whitened, precision=highest, preferred_element_type=jnp.f...  25.8 us
    dot_general x1, matrix products, per_device(): jnp.dot(kernel, whitening, precision=highest, preferred_element_type=jnp....  16.3 us
  transfers between devices with their start and end apart: 3, of which 3 were waited for; matrix products, arithmetic and copies ran while one was open for 0% of the time, Pallas kernels for 0%

commit v1 on v0

v1 whole, which is shorter than its diff:
```python
import functools

import jax
import jax.numpy as jnp
from jax import lax
from jax.experimental import pallas as pl
from jax.experimental.pallas import tpu as pltpu
from jax.sharding import PartitionSpec as P

SPREAD = 51
CLUSTERS = 4096

f32, bf16 = jnp.float32, jnp.bfloat16
MESH = pl.DeviceIdType.MESH


def nn(a, b):
    return lax.dot_general(a, b, (((1,), (0,)), ((), ())), preferred_element_type=f32)


def nt(a, b):
    return lax.dot_general(a, b, (((1,), (1,)), ((), ())), preferred_element_type=f32)


def split(x):
    high = x.astype(bf16)
    return high, (x - high.astype(f32)).astype(bf16)


def ones_where(mask):
    return jnp.where(mask, 1.0, 0.0).astype(bf16)


def iota(shape, axis):
    return lax.broadcasted_iota(jnp.int32, shape, axis)


def kernel(slots, dense, points_ref, centres_ref, white_ref, assign_ref, out_ref,
           feats, wfull, wh, wl, dh, dl, lh, ll, pick, fold, pos, kh, kl, ah, al,
           sbuf, rbuf, local_sem, gs, gr, fs, fr, zs, zr):
    rows = assign_ref.shape[1]
    part = points_ref.shape[1]
    centres = centres_ref.shape[1]
    cols = white_ref.shape[1]
    owned = out_ref.shape[0]
    half = slots // 2
    z, c, p = lax.axis_index("row"), lax.axis_index("col"), lax.axis_index("rep")
    nz = lax.axis_size("row")
    xh, y, core = c // 8, lax.rem(c // 2, 4), lax.rem(c, 2)
    sibling = {"row": z, "col": c + 1 - 2 * core, "rep": p}
    ahead = {"row": lax.rem(z + 1, nz), "col": c, "rep": p}
    behind = {"row": lax.rem(z + nz - 1, nz), "col": c, "rep": p}

    def slot(col, rep, both):
        start = rep * part if both else rep * (part + centres)
        return feats.at[pl.ds(pl.multiple_of(col * 16, 16), 16),
                        pl.ds(pl.multiple_of(start, 128), part + centres if both else part)]

    def peer(a, b, dy):
        px = a + xh - 2 * a * xh
        return px * 8 + lax.rem(y + dy, 4) * 2 + core, b + p - 2 * b * p

    own_points = pltpu.make_async_copy(points_ref, slot(c, p, False), local_sem.at[0])
    own_centres = pltpu.make_async_copy(
        centres_ref, feats.at[pl.ds(pl.multiple_of(c * 16, 16), 16), pl.ds(part, centres)], local_sem.at[1])
    own_white = pltpu.make_async_copy(white_ref, wfull, local_sem.at[2])
    own_points.start()
    own_centres.start()
    own_white.start()

    barrier = pltpu.get_barrier_semaphore()
    others = [(a, b, dy) for dy in range(4) for a in range(2) for b in range(2) if (a, b, dy) != (0, 0, 0)]
    for a, b, dy in others:
        col, rep = peer(a, b, dy)
        pl.semaphore_signal(barrier, inc=1, device_id={"row": z, "col": col, "rep": rep}, device_id_type=MESH)
    for target in (sibling, ahead, behind):
        pl.semaphore_signal(barrier, inc=1, device_id=target, device_id_type=MESH)
    pl.semaphore_wait(barrier, len(others) + 3)

    own_points.wait()
    own_centres.wait()

    def gather(a, b, dy):
        index = (a * 2 + b) * 4 + dy
        col, rep = peer(a, b, dy)
        mine = slot(c, p, a == b)
        return pltpu.make_async_remote_copy(mine, mine, gs.at[index], gr.at[index],
                                            device_id={"row": z, "col": col, "rep": rep}, device_id_type=MESH)

    def arrival(a, b, dy, both):
        index = (a * 2 + b) * 4 + dy
        col, rep = peer(a, b, 4 - dy)
        theirs = slot(col, rep, both)
        return (pltpu.make_async_remote_copy(theirs, theirs, gs.at[index], gr.at[index],
                                             device_id=sibling, device_id_type=MESH),
                pltpu.make_async_remote_copy(theirs, theirs, fs.at[index], fr.at[index],
                                             device_id=sibling, device_id_type=MESH))

    def handed(a, b, dy, both):
        index = (a * 2 + b) * 4 + dy
        col, rep = peer(a, b, 4 - dy)
        theirs = slot(col + 1 - 2 * core, rep, both)
        return pltpu.make_async_remote_copy(theirs, theirs, fs.at[index], fr.at[index],
                                            device_id=sibling, device_id_type=MESH)

    for a, b, dy in others:
        gather(a, b, dy).start()
    arrival(0, 0, 0, True)[1].start()

    own_white.wait()

    @pl.loop(0, centres // 128)
    def _(i):
        at = pl.ds(pl.multiple_of(i * 128, 128), 128)
        high, low = split(wfull[at, :])
        wh[at, :] = high
        wl[at, :] = low

    assign = assign_ref[...]
    owner_of = assign // owned

    def owner_at(j):
        far = nz // 2 - (j + 1) // 2
        step = jnp.where(lax.rem(j, 2) == 1, far, nz - far) if not isinstance(j, int) else (far if j % 2 else nz - far)
        return lax.rem(z + step, nz) * 2 + p

    def members(owner):
        return ones_where(iota((owned, rows), 0) == assign - owner * owned)

    if not dense:
        before = ones_where(iota((128, 128), 0) < iota((128, 128), 1))
        base = jnp.zeros((16, 1), f32)
        for block in range(rows // 128):
            at = pl.ds(block * 128, 128)
            mine = ones_where(iota((16, 128), 0) == owner_of[:, block * 128:(block + 1) * 128])
            mine32 = mine.astype(f32)
            pos[:, at] = jnp.sum(mine32 * (nn(mine, before) + base), axis=0, keepdims=True)
            base = base + jnp.sum(mine32, axis=1, keepdims=True)
        below = ones_where(iota((owned, owned), 0) < iota((owned, owned), 1))

    def prepare(j):
        owner = owner_at(j)
        take = fold.shape[2]
        rank = jnp.where(owner_of == owner, pos[...], -1.0).astype(jnp.int32)
        chosen = ones_where(iota((take, rows), 0) == rank)
        pick[j] = chosen
        belongs = members(owner)
        counts = nt(jnp.ones((8, rows), bf16), belongs)
        active = counts > 0.5
        order = nn(ones_where(active), below).astype(jnp.int32)
        squeeze = ones_where((iota((slots, owned), 0) == order[0:1]) & active[0:1])
        fold[j] = nn(squeeze, nt(belongs, chosen).astype(bf16)).astype(bf16)

    def pass_on(j):
        dy = lax.rem(j, 4)
        a = j // 4

        @pl.when(j > 0)
        def _():
            got, on = arrival(a, a, dy, True)
            got.wait_recv()
            on.start()

        got, on = arrival(a, 1 - a, dy, False)
        got.wait_recv()
        on.start()

    @pl.loop(0, 8)
    def _(j):
        if not dense:
            prepare(j)
        pass_on(j)

    @pl.loop(0, 8)
    def _(j):
        dy = lax.rem(j, 4)
        a = j // 4
        handed(a, a, dy, True).wait_recv()
        handed(a, 1 - a, dy, False).wait_recv()

    squares = jnp.zeros((1, centres), f32)
    for i in range(8):
        at = pl.ds(i * 32, 32)
        centre = feats[at, part:part + centres]
        squares = squares + jnp.sum(centre * centre, axis=0, keepdims=True)
        lh[at, :], ll[at, :] = split(centre)
        dh[at, :part], dl[at, :part] = split(feats[at, :part])
        dh[at, part:], dl[at, part:] = split(feats[at, part + centres:])

    def kernel_rows(xhi, xlo, at):
        x = xhi + xlo
        norm = jnp.sum(x * x, axis=1, keepdims=True)
        xhi, xlo = xhi.astype(bf16), xlo.astype(bf16)
        for i in range(centres // 512):
            on = slice(i * 512, (i + 1) * 512)
            inner = nn(xhi, lh[:, on]) + nn(xhi, ll[:, on]) + nn(xlo, lh[:, on])
            value = jnp.exp((norm + squares[:, on] - 2.0 * inner) * (-1.0 / (2.0 * SPREAD)))
            kh[at, on], kl[at, on] = split(value)

    if dense:
        eye = ones_where(iota((256, 256), 0) == iota((256, 256), 1))

        @pl.loop(0, rows // 256)
        def _(i):
            at = pl.ds(pl.multiple_of(i * 256, 256), 256)
            kernel_rows(nt(eye, dh[:, at]), nt(eye, dl[:, at]), at)

    def blocks(first, count):
        if not dense:
            take = fold.shape[2]
            for i in range(count):
                chosen = pick[first + i]
                kernel_rows(nt(chosen, dh[...]), nt(chosen, dl[...]), slice(i * take, (i + 1) * take))
        for i in range(count):
            at = slice(i * slots, (i + 1) * slots)
            if dense:
                chosen, on = members(owner_at(first + i)), slice(0, rows)
            else:
                chosen, on = fold[first + i], slice(i * take, (i + 1) * take)
            for k in range(centres // 512):
                lanes = slice(k * 512, (k + 1) * 512)
                ah[at, lanes], al[at, lanes] = split(nn(chosen, kh[on, lanes]) + nn(chosen, kl[on, lanes]))
        every = slice(0, count * slots)
        return nn(ah[every, :], wh[...]) + nn(ah[every, :], wl[...]) + nn(al[every, :], wh[...])

    def hop(way, step, part_of):
        at = pl.ds(part_of * half, half)
        return pltpu.make_async_remote_copy(sbuf.at[way, step, at], rbuf.at[way, step, at],
                                            zs.at[way, step, part_of], zr.at[way, step, part_of],
                                            device_id=(ahead, behind)[way], device_id_type=MESH)

    made = blocks(0, 1)
    sbuf[0, 0, :half] = made[:half]
    sbuf[1, 0, half:] = made[half:]
    hop(0, 0, 0).start()
    hop(1, 0, 1).start()
    for step in range(1, 4):
        made = blocks(2 * step - 1, 2)
        sbuf[0, step] = made[:slots]
        sbuf[1, step] = made[slots:]
        for turn in range(2):
            for way in range(2):
                part_of = (1 - way if turn == 0 else way) if step == 1 else turn
                at = pl.ds(part_of * half, half)
                if step > 1 or turn == 1:
                    hop(way, step - 1, part_of).wait_recv()
                    sbuf[way, step, at] += rbuf[way, step - 1, at]
                hop(way, step, part_of).start()
    made = blocks(7, 1)
    if not dense:
        belongs = members(lax.rem(z, nz) * 2 + p)
        counts = nn(belongs, jnp.ones((rows, slots), bf16))
        order = nn(ones_where(iota((owned, owned), 0) > iota((owned, owned), 1)), ones_where(counts > 0.5))
        spread = ones_where((order.astype(jnp.int32) == iota((owned, slots), 1)) & (counts > 0.5))
    for way in range(2):
        for part_of in range(2):
            hop(way, 3, part_of).wait_recv()
    total = made + rbuf[0, 3] + rbuf[1, 3]
    if dense:
        out_ref[...] = total
    else:
        high, low = split(total)
        rest = (total - high.astype(f32) - low.astype(f32)).astype(bf16)
        out_ref[...] = nn(spread, high) + nn(spread, low) + nn(spread, rest)

    for a, b, dy in others:
        gather(a, b, dy).wait_send()
    for j in range(8):
        a, dy = j // 4, j % 4
        arrival(a, a, dy, True)[1].wait_send()
        arrival(a, 1 - a, dy, False)[1].wait_send()
    for way in range(2):
        for step in range(4):
            for part_of in range(2):
                if step > 0 or part_of == way:
                    hop(way, step, part_of).wait_send()


def call(slots, take, dense, points, centres, white, assign):
    features, part = points.shape[0] * lax.axis_size("col"), points.shape[1]
    count, cols = white.shape
    rows = assign.shape[1]
    owned = CLUSTERS // (lax.axis_size("row") * lax.axis_size("rep"))
    held = rows if dense else 2 * take
    dma = pltpu.SemaphoreType.DMA
    small = dense
    return pl.pallas_call(
        functools.partial(kernel, slots, dense),
        out_shape=jax.ShapeDtypeStruct((owned, cols), f32),
        in_specs=[pl.BlockSpec(memory_space=pl.ANY)] * 3 + [pl.BlockSpec(memory_space=pltpu.VMEM)],
        out_specs=pl.BlockSpec(memory_space=pltpu.VMEM),
        scratch_shapes=[
            pltpu.VMEM((features, 2 * part + count), f32),
            pltpu.VMEM((count, cols), f32),
            pltpu.VMEM((count, cols), bf16),
            pltpu.VMEM((count, cols), bf16),
            pltpu.VMEM((features, rows), bf16),
            pltpu.VMEM((features, rows), bf16),
            pltpu.VMEM((features, count), bf16),
            pltpu.VMEM((features, count), bf16),
            pltpu.VMEM((8, 16, 128) if small else (8, take, rows), bf16),
            pltpu.VMEM((8, 16, 128) if small else (8, slots, take), bf16),
            pltpu.VMEM((1, rows), f32),
            pltpu.VMEM((held, count), bf16),
            pltpu.VMEM((held, count), bf16),
            pltpu.VMEM((2 * slots, count), bf16),
            pltpu.VMEM((2 * slots, count), bf16),
            pltpu.VMEM((2, 4, slots, cols), f32),
            pltpu.VMEM((2, 4, slots, cols), f32),
            dma((3,)), dma((16,)), dma((16,)), dma((16,)), dma((16,)),
            dma((2, 4, 2)), dma((2, 4, 2)),
        ],
        compiler_params=pltpu.CompilerParams(
            collective_id=1 if dense else 0, has_side_effects=True, vmem_limit_bytes=60 * 2**20),
    )(points, centres, white, assign)


def per_device(descriptors, landmarks, whitening, assign):
    return call(256, 256, True, descriptors.T, landmarks.T, whitening, assign.reshape(1, -1))


def solution(mesh):
    placed = (P("rep", "col"), P("row", "col"), P("row", "col"), P())
    return jax.shard_map(
        per_device, mesh=mesh, in_specs=placed, out_specs=P(("row", "rep"), "col"), check_vma=False
    )
```

time: 441 us -> 120 us (0.27)
  waiting for transfers between devices: 375 us -> 0 us
  Pallas kernels: 0 us -> 118 us
  matrix products: 49.4 us -> 0 us
  between operations: 13.2 us -> 0.01 us
    reduce_scatter x1 -> x0, waiting for transfers between devices: 266 us -> none  [per_device(): lax.psum_scatter(jnp.dot(onehot, whitened, precision=highest, preferred_e...]
    pallas_call x0 -> x1, Pallas kernels: none -> 118 us  [call(): pl.pallas_call(functools.partial(kernel, slots, dense), out_shape=jax.Sha...]
    all_gather x2 -> x0, waiting for transfers between devices: 108 us -> none  [the longest x1 56.2 us: per_device(): lax.all_gather(descriptors, 'col', axis=1, tiled=True)]
    dot_general x3 -> x0, matrix products: 49.4 us -> none  [the longest x1 25.8 us: per_device(): jnp.dot(onehot, whitened, precision=highest, preferred_element_type=jnp.f...]
  transfers between devices with their start and end apart: 3 -> 0, of which waited for: 3 -> 0; matrix products, arithmetic and copies ran while one was open for 0% -> 0% of each run, Pallas kernels for 0% -> 0%
where the time goes in v1:
time: 120 us
  Pallas kernels  118 us (98%)
  local copies, waits for them, and re-layouts  2.06 us (2%)
    pallas_call x1, Pallas kernels, call(): pl.pallas_call(functools.partial(kernel, slots, dense), out_shape=jax.Sha...  118 us

profile of v1, /device:TPU:1, one launch (start us, length us, event | category | flops | bytes accessed | tf_op | source)
XLA Modules:
  0.0 119.7 jit_solution(8422146073530878793)
XLA Ops:
  0.0 117.6 %shard_map.46 = f32[256,768]{1,0:T(8,128)} custom-call(f32[16,1024]{1,0:T(8,128)} %bitcast.4, f32[16,1536]{1,0:T(8,128)} %bitcast.3, f32[1536,768]{1,0:T(8,128)} %white_ref.1, s32[1,2048]{1,0:T(1,128)} %bitcast.5), custom_call_target="tpu_custom_call" | custom-call | tf_op jit(solution)/shard_map/pallas_call | solution.py:287
  117.6 2.1 %copy.6 = f32[256,768]{1,0:T(8,128)} copy(f32[256,768]{1,0:T(8,128)} %shard_map.46) | data formatting | bytes 1572864
